TPU v7x, 128 devices: a whole 4x4x4 slice. The times are simulated.
128 devices in a mesh: tm: 16 (over y, x), orb: 8 (over z, core).
Axes of the slice: x: 4, y: 4, z: 4, core: 2. Of those that a mesh axis runs over, the one named last changes fastest.
Arguments:
- forward: bfloat16 [2, 2, 512, 128, 128], P(None, None, 'tm'), may hold values from -2 to 2
- backward_slab: bfloat16 [2, 2, 512, 128, 128], P(None, None, 'tm', 'orb'), may hold values from -2 to 2
- slot_time: int32 [512], replicated, may hold values from 0 to 511, as said below
- pattern: int32 [128, 128], replicated, may hold values 0 or 1
- coupling: float32 [128, 128], replicated, may hold values from -1 to 1
- hamiltonian: float32 [128, 128], replicated, may hold values from -0.8 to 0.8
- lesser_now: float32 [2, 128, 128], replicated, may hold values from -1.5 to 1.5
Outputs:
- lesser_next: float32 [2, 128, 128], P(None, 'orb')
Inputs may be any that keep to these rules, and one draw needn't show every extreme that they name: slot_time is a permutation of the 512 history times. The 32 slots of each index d of tm hold exactly 32 // 16 times of the range [e * 32, (e + 1) * 32) for every index e of tm.
All inputs are finite; a program needn't handle non-finite values.
Results may differ from a plain program's by a relative error of at most 0.0054.
Values may be sent and summed in bfloat16 or wider, within the bound.
No kernel may reach another device: no remote copies, remote signals or barrier semaphores. Data moves between devices by JAX's collectives and lax.ppermute only.
A program may use at most 64 MiB of HBM per device.

v0:
```python
import math
import jax
import jax.numpy as jnp
from jax import lax
from jax.sharding import PartitionSpec as P

history_step = 0.02
update_step = 0.5


def complex_einsum(form, left_re, left_im, right_re, right_im):
    real_part = jnp.einsum(
        form, left_re, right_re, preferred_element_type=jnp.float32
    ) - jnp.einsum(form, left_im, right_im, preferred_element_type=jnp.float32)
    imag_part = jnp.einsum(
        form, left_re, right_im, preferred_element_type=jnp.float32
    ) + jnp.einsum(form, left_im, right_re, preferred_element_type=jnp.float32)
    return (real_part, imag_part)


def self_energy(fwd_re, fwd_im, back_re, back_im, interaction, inter_rows, row_start, row_count):
    rows_re = lax.dynamic_slice_in_dim(fwd_re, row_start, row_count, 1)
    rows_im = lax.dynamic_slice_in_dim(fwd_im, row_start, row_count, 1)
    fwd_re32 = fwd_re.astype(jnp.float32)
    fwd_im32 = fwd_im.astype(jnp.float32)
    trans_re = jnp.swapaxes(back_re, 1, 2).astype(jnp.float32)
    trans_im = jnp.swapaxes(back_im, 1, 2).astype(jnp.float32)
    bubble_re = (fwd_re32 * trans_re - fwd_im32 * trans_im).astype(jnp.bfloat16)
    bubble_im = (fwd_re32 * trans_im + fwd_im32 * trans_re).astype(jnp.bfloat16)
    left_re = jnp.einsum(
        "ik,skj->sij", inter_rows, bubble_re, preferred_element_type=jnp.float32
    ).astype(jnp.bfloat16)
    left_im = jnp.einsum(
        "ik,skj->sij", inter_rows, bubble_im, preferred_element_type=jnp.float32
    ).astype(jnp.bfloat16)
    screen_re = jnp.einsum("sik,kj->sij", left_re, interaction, preferred_element_type=jnp.float32)
    screen_im = jnp.einsum("sik,kj->sij", left_im, interaction, preferred_element_type=jnp.float32)
    rows_re32 = rows_re.astype(jnp.float32)
    rows_im32 = rows_im.astype(jnp.float32)
    direct_re = rows_re32 * screen_re - rows_im32 * screen_im
    direct_im = rows_re32 * screen_im + rows_im32 * screen_re
    inter_rows32 = inter_rows.astype(jnp.float32)
    scaled_re = (inter_rows32[None, :, :, None] * fwd_re32[:, None]).astype(jnp.bfloat16)
    scaled_im = (inter_rows32[None, :, :, None] * fwd_im32[:, None]).astype(jnp.bfloat16)
    inner_re, inner_im = complex_einsum("slm,simj->silj", back_re, back_im, scaled_re, scaled_im)
    inter32 = interaction.astype(jnp.float32)
    weighted_re = (inner_re * inter32).astype(jnp.bfloat16)
    weighted_im = (inner_im * inter32).astype(jnp.bfloat16)
    exch_re, exch_im = complex_einsum("sil,silj->sij", rows_re, rows_im, weighted_re, weighted_im)
    sigma_re = (direct_re - exch_re).astype(jnp.bfloat16)
    sigma_im = (direct_im - exch_im).astype(jnp.bfloat16)
    return (sigma_re, sigma_im)


def block_terms(fwd_block, back_block, weights, interaction, inter_rows, row_start, row_count):
    summed = None
    scale = weights[:, None, None]
    for branch in (0, 1):
        other = 1 - branch
        factor = 1.0 if branch == 0 else -1.0
        sigma_re, sigma_im = self_energy(
            fwd_block[branch, 0],
            fwd_block[branch, 1],
            back_block[other, 0],
            back_block[other, 1],
            interaction,
            inter_rows,
            row_start,
            row_count,
        )
        prod_re, prod_im = complex_einsum(
            "sil,slj->sij", sigma_re, sigma_im, back_block[other, 0], back_block[other, 1]
        )
        term = factor * jnp.stack(
            [jnp.sum(scale * prod_re, axis=0), jnp.sum(scale * prod_im, axis=0)]
        )
        summed = term if summed is None else summed + term
    return summed


def history_terms(fwd_part, back_part, weights, interaction, inter_rows, row_start, row_count):
    slices_here = fwd_part.shape[2]
    block_size = math.gcd(max(4, 128 // row_count), slices_here)
    block_count = slices_here // block_size
    orbitals = fwd_part.shape[3]

    def add_block(block, running):
        start = block * block_size
        fwd_block = lax.dynamic_slice_in_dim(fwd_part, start, block_size, 2)
        back_block = lax.dynamic_slice_in_dim(back_part, start, block_size, 2)
        weight_block = lax.dynamic_slice_in_dim(weights, start, block_size, 0)
        return running + block_terms(
            fwd_block, back_block, weight_block, interaction, inter_rows, row_start, row_count
        )

    initial = jnp.zeros((2, row_count, orbitals), jnp.float32)
    return lax.fori_loop(0, block_count, add_block, initial)


def on_device(forward, backward_slab, slot_time, pattern, coupling, hamiltonian, lesser_now):
    tm_count = lax.axis_size("tm")
    my_time = lax.axis_index("tm")
    my_orb = lax.axis_index("orb")
    per_device = forward.shape[2]
    row_count = backward_slab.shape[3]
    per_peer = per_device // tm_count
    slices_all = per_device * tm_count
    row_start = my_orb * row_count
    time_start = my_time * per_device
    holder_of = slot_time // per_device
    my_holders = lax.dynamic_slice_in_dim(holder_of, time_start, per_device)
    send_order = jnp.argsort(my_holders, stable=True)
    sorted_slab = jnp.take(backward_slab, send_order, axis=2)
    holder_grid = holder_of.reshape(tm_count, per_device)
    time_grid = slot_time.reshape(tm_count, per_device)
    not_mine = (holder_grid != my_time).astype(jnp.int32)
    positions = jnp.argsort(not_mine, axis=1, stable=True)[:, :per_peer]
    times_here = jnp.take_along_axis(time_grid, positions, axis=1).reshape(per_device)
    natural = jnp.argsort(times_here - time_start)
    masked = coupling * pattern.astype(jnp.float32)
    interaction = ((masked + masked.T) * 0.5).astype(jnp.bfloat16)
    inter_rows = lax.dynamic_slice_in_dim(interaction, row_start, row_count, 0)
    time_index = time_start + jnp.arange(per_device, dtype=jnp.int32)
    edges = (time_index == 0) | (time_index == slices_all - 1)
    weights = jnp.where(edges, jnp.float32(0.5), jnp.float32(1.0)) * history_step
    full_sorted = lax.all_gather(sorted_slab, "orb", axis=3, tiled=True)
    arrived = lax.all_to_all(full_sorted, "tm", split_axis=2, concat_axis=2, tiled=True)
    back_full = jnp.take(arrived, natural, axis=2)
    local_collision = history_terms(
        forward, back_full, weights, interaction, inter_rows, row_start, row_count
    )
    summed_rows = lax.psum(local_collision, "tm")
    collision = lax.all_gather(summed_rows, "orb", axis=1, tiled=True)
    own_rows = lax.dynamic_slice_in_dim(collision, row_start, row_count, 1)
    own_columns = lax.dynamic_slice_in_dim(collision, row_start, row_count, 2)
    herm_re = own_rows[0] + own_columns[0].T
    herm_im = own_rows[1] - own_columns[1].T
    high = lax.Precision.HIGHEST
    ham_rows = lax.dynamic_slice_in_dim(hamiltonian, row_start, row_count, 0)
    lesser_rows = lax.dynamic_slice_in_dim(lesser_now, row_start, row_count, 1)
    comm_re = jnp.dot(ham_rows, lesser_now[0], precision=high) - jnp.dot(
        lesser_rows[0], hamiltonian, precision=high
    )
    comm_im = jnp.dot(ham_rows, lesser_now[1], precision=high) - jnp.dot(
        lesser_rows[1], hamiltonian, precision=high
    )
    next_re = lesser_rows[0] + update_step * (comm_im + herm_im)
    next_im = lesser_rows[1] - update_step * (comm_re + herm_re)
    return jnp.stack([next_re, next_im])


def solution(mesh):
    in_specs = (
        P(None, None, "tm", None, None),
        P(None, None, "tm", "orb", None),
        P(),
        P(),
        P(),
        P(),
        P(),
    )
    out_specs = P(None, "orb", None)
    return jax.shard_map(
        on_device, mesh=mesh, in_specs=in_specs, out_specs=out_specs, check_vma=False
    )
```

profile of v0, /device:TPU:1, one launch (start us, length us, event | category | flops | bytes accessed | tf_op | source)
XLA Modules:
  0.0 479.0 jit_solution(11907473625283810762)
XLA Ops:
  10.6 39.5 %all-gather.2.cloned.1.call-done = bf16[2,2,32,128,128]{4,3,1,0,2:T(8,128)(2,1)} async-done(((bf16[2,2,32,16,128]{4,3,1,0,2:T(8,128)(2,1)}), bf16[2,2,32,128,128]{4,3,1,0,2:T(8,128)(2,1)}) %all-gather.2.cloned.1.call-update) | async-done | bytes 4194320 | tf_op jit(solution)/shard_map/all_gather | solution.py:126
  50.1 6.6 %all-to-all-start = ((bf16[2,2,32,128,128]{4,3,1,0,2:T(8,128)(2,1)}), bf16[2,2,32,128,128]{4,3,1,0,2:T(8,128)(2,1)}, u32[]{:S(2)}, u32[]{:S(2)}) async-start(bf16[2,2,32,128,128]{4,3,1,0,2:T(8,128)(2,1)} %all-gather.2.cloned.1.call-done), calls=%async_computation | async-start | bytes 8388608 | tf_op jit(solution)/shard_map/all_to_all | solution.py:127
  64.0 55.6 %all-to-all-done = bf16[2,2,32,128,128]{4,3,1,0,2:T(8,128)(2,1)} async-done(((bf16[2,2,32,128,128]{4,3,1,0,2:T(8,128)(2,1)}), bf16[2,2,32,128,128]{4,3,1,0,2:T(8,128)(2,1)}, u32[]{:S(2)}, u32[]{:S(2)}) %all-to-all-start) | async-done | bytes 4194336 | tf_op jit(solution)/shard_map/all_to_all | solution.py:127
  119.6 4.7 copy.45
  124.3 5.2 %gather_fusion.1 = bf16[32,2,2,128,128]{4,3,2,1,0:T(8,128)(2,1)} fusion(bf16[2,2,32,128,128]{4,3,2,1,0:T(8,128)(2,1)} %copy.45, s32[1024]{0:T(1024)S(1)} %pad_clamp_fusion), kind=kCustom, calls=%fused_computation.1 | custom fusion | bytes 8388736 | tf_op jit(solution)/shard_map/jit(_take)/gather | solution.py:128
  129.5 4.6 select_bitcast_fusion
  134.1 249.0 %while.16 = (s32[]{:T(128)}, f32[2,16,128]{2,1,0:T(8,128)}, f32[32]{0:T(128)S(1)}, bf16[2,2,32,128,128]{4,3,2,1,0:T(8,128)(2,1)}, s32[]{:T(128)}, /*index=5*/bf1...) while((s32[]{:T(128)}, f32[2,16,128]{2,1,0:T(8,128)}, ...), condition=%wide.region_8.9_spmd.clone, body=%wide.region_3.8_spmd.clone.sunk | while | flops 4459808768 | bytes 142112496 | solution.py:97
  148.4 2.6 fusion.413
  153.3 2.3 fusion.414
  157.8 2.6 fusion.410
  162.7 2.3 fusion.411
  173.2 2.6 fusion.427
  178.1 2.3 fusion.428
  182.5 2.6 fusion.424
  187.5 2.3 fusion.425
  210.6 2.6 fusion.413
  215.5 2.3 fusion.414
  220.0 2.6 fusion.410
  224.9 2.3 fusion.411
  235.4 2.6 fusion.427
  240.3 2.3 fusion.428
  244.8 2.6 fusion.424
  272.9 2.6 fusion.413
  282.3 2.6 fusion.410
  297.6 2.6 fusion.427
  307.0 2.6 fusion.424
  335.1 2.6 fusion.413
  344.5 2.6 fusion.410
  359.9 2.6 fusion.427
  369.3 2.6 fusion.424
  383.1 58.1 %psum.7 = f32[2,16,128]{2,1,0:T(8,128)S(1)} all-reduce(f32[2,16,128]{2,1,0:T(8,128)} %get-tuple-element.204), channel_id=1, replica_groups=mesh['tm'=16,'orb'=8] {'tm'}, use_global_device_ids=true, to_apply=%region_9.10 | all-reduce | flops 4096 | bytes 32768 | tf_op jit(solution)/shard_map/psum | solution.py:132
  441.1 28.1 %all_gather.7 = f32[2,128,128]{2,1,0:T(8,128)S(1)} all-gather(f32[2,16,128]{2,1,0:T(8,128)S(1)} %psum.7), channel_id=1, replica_groups=mesh['tm'=16,'orb'=8] {'orb'}, dimensions={1}, use_global_device_ids=true | all-gather | bytes 147456 | tf_op jit(solution)/shard_map/all_gather | solution.py:133
  (287 shorter events, 204.2 us)
Async XLA Ops:
  6.5 2.5 copy-start
  6.5 43.6 %all-gather.2.cloned.1.call-start = ((), (), s32[]{:S(2)}) async-start(), calls=%async_computation.1 | async-start | bytes 4718592 | tf_op jit(solution)/shard_map/all_gather | solution.py:126
  10.6 46.1 %copy-start.11 = (s32[512]{0:T(512)S(1)}, s32[512]{0:T(512)}, u32[]{:S(2)}) copy-start(s32[512]{0:T(512)} %param.11) | copy-start | bytes 6148
  50.1 69.5 %all-to-all-start = ((bf16[2,2,32,128,128]{4,3,1,0,2:T(8,128)(2,1)}), bf16[2,2,32,128,128]{4,3,1,0,2:T(8,128)(2,1)}, u32[]{:S(2)}, u32[]{:S(2)}) async-start(bf16[2,2,32,128,128]{4,3,1,0,2:T(8,128)(2,1)} %all-gather.2.cloned.1.call-done), calls=%async_computation | async-start | bytes 8388608 | tf_op jit(solution)/shard_map/all_to_all | solution.py:127
  57.9 1.1 copy-start.9
  58.0 1.2 copy-start.10
  58.0 3.1 copy-start.8
  134.1 6.7 %copy-start.2 = (bf16[128,128]{1,0:T(8,128)(2,1)}, bf16[128,128]{1,0:T(8,128)(2,1)S(1)}, u32[]{:S(2)}) copy-start(bf16[128,128]{1,0:T(8,128)(2,1)S(1)} %get-tuple-element.394) | copy-start | bytes 98308 | tf_op jit(solution)/shard_map/while
  160.4 4.5 copy-start.5
  185.2 4.5 copy-start.3
  185.2 4.5 copy-start.4
  187.5 8.3 %copy-start.6 = (f32[2,16,128]{2,1,0:T(8,128)S(1)}, f32[2,16,128]{2,1,0:T(8,128)}, u32[]{:S(2)}) copy-start(f32[2,16,128]{2,1,0:T(8,128)} %get-tuple-element.375) | copy-start | bytes 49156 | tf_op jit(solution)/shard_map/while
  187.5 8.9 %copy-start.13 = (f32[32]{0:T(128)S(1)}, f32[32]{0:T(128)}, u32[]{:S(2)}) copy-start(f32[32]{0:T(128)} %copy-done.12) | copy-start | bytes 388 | tf_op jit(solution)/shard_map/while
  196.4 6.7 %copy-start.2 = (bf16[128,128]{1,0:T(8,128)(2,1)}, bf16[128,128]{1,0:T(8,128)(2,1)S(1)}, u32[]{:S(2)}) copy-start(bf16[128,128]{1,0:T(8,128)(2,1)S(1)} %get-tuple-element.394) | copy-start | bytes 98308 | tf_op jit(solution)/shard_map/while
  222.7 4.5 copy-start.5
  247.4 4.5 copy-start.3
  247.4 4.5 copy-start.4
  249.7 8.3 %copy-start.6 = (f32[2,16,128]{2,1,0:T(8,128)S(1)}, f32[2,16,128]{2,1,0:T(8,128)}, u32[]{:S(2)}) copy-start(f32[2,16,128]{2,1,0:T(8,128)} %get-tuple-element.375) | copy-start | bytes 49156 | tf_op jit(solution)/shard_map/while
  249.7 8.9 %copy-start.13 = (f32[32]{0:T(128)S(1)}, f32[32]{0:T(128)}, u32[]{:S(2)}) copy-start(f32[32]{0:T(128)} %copy-done.12) | copy-start | bytes 388 | tf_op jit(solution)/shard_map/while
  258.6 6.7 %copy-start.2 = (bf16[128,128]{1,0:T(8,128)(2,1)}, bf16[128,128]{1,0:T(8,128)(2,1)S(1)}, u32[]{:S(2)}) copy-start(bf16[128,128]{1,0:T(8,128)(2,1)S(1)} %get-tuple-element.394) | copy-start | bytes 98308 | tf_op jit(solution)/shard_map/while
  284.9 4.5 copy-start.5
  309.7 4.5 copy-start.3
  309.7 4.5 copy-start.4
  311.9 8.3 %copy-start.6 = (f32[2,16,128]{2,1,0:T(8,128)S(1)}, f32[2,16,128]{2,1,0:T(8,128)}, u32[]{:S(2)}) copy-start(f32[2,16,128]{2,1,0:T(8,128)} %get-tuple-element.375) | copy-start | bytes 49156 | tf_op jit(solution)/shard_map/while
  311.9 8.9 %copy-start.13 = (f32[32]{0:T(128)S(1)}, f32[32]{0:T(128)}, u32[]{:S(2)}) copy-start(f32[32]{0:T(128)} %copy-done.12) | copy-start | bytes 388 | tf_op jit(solution)/shard_map/while
  320.8 6.7 %copy-start.2 = (bf16[128,128]{1,0:T(8,128)(2,1)}, bf16[128,128]{1,0:T(8,128)(2,1)S(1)}, u32[]{:S(2)}) copy-start(bf16[128,128]{1,0:T(8,128)(2,1)S(1)} %get-tuple-element.394) | copy-start | bytes 98308 | tf_op jit(solution)/shard_map/while
  347.1 4.5 copy-start.5
  371.9 4.5 copy-start.3
  371.9 4.5 copy-start.4
  374.2 8.3 %copy-start.6 = (f32[2,16,128]{2,1,0:T(8,128)S(1)}, f32[2,16,128]{2,1,0:T(8,128)}, u32[]{:S(2)}) copy-start(f32[2,16,128]{2,1,0:T(8,128)} %get-tuple-element.375) | copy-start | bytes 49156 | tf_op jit(solution)/shard_map/while
  374.2 8.9 %copy-start.13 = (f32[32]{0:T(128)S(1)}, f32[32]{0:T(128)}, u32[]{:S(2)}) copy-start(f32[32]{0:T(128)} %copy-done.12) | copy-start | bytes 388 | tf_op jit(solution)/shard_map/while
  383.1 89.1 %copy-start.1 = (bf16[2,2,32,16,128]{4,3,2,1,0:T(8,128)(2,1)S(1)}, bf16[2,2,32,16,128]{4,3,2,1,0:T(8,128)(2,1)}, u32[]{:S(2)}) copy-start(bf16[2,2,32,16,128]{4,3,2,1,0:T(8,128)(2,1)} %param.10) | copy-start | bytes 1572868
  (8 other events, 4.4 us)
Sparse Core Ops, SparseCore 0:
  10.7 39.3 all-gather.1
where the time goes:
time: 482 us; the launch traced here: 479 us
  matrix products  219 us (45%)
  waiting for transfers between devices  95.1 us (20%)
  blocking collectives  86.2 us (18%)
  local copies, waits for them, and re-layouts  46.3 us (10%)
  between operations  13.6 us (3%)
  other arithmetic  11.6 us (2%)
  starting transfers between devices  6.58 us (1%)
    psum x1, blocking collectives, on_device(): summed_rows = lax.psum(local_collision, 'tm')  58.1 us
    all_to_all x1, waiting for transfers between devices, on_device(): lax.all_to_all(full_sorted, 'tm', split_axis=2, concat_axis=2, tiled=True)  55.6 us
    dot_general x24, matrix products, complex_einsum(): jnp.einsum(form, left_re, right_im, preferred_element_type=jnp.float32)  48.3 us
    dot_general x24, matrix products, complex_einsum(): jnp.einsum(form, left_im, right_im, preferred_element_type=jnp.float32)  48.2 us
    dot_general x24, matrix products, complex_einsum(): jnp.einsum(form, left_im, right_re, preferred_element_type=jnp.float32)  45 us
    dot_general x24, matrix products, complex_einsum(): jnp.einsum(form, left_re, right_re, preferred_element_type=jnp.float32)  44.8 us
    all_gather x1, waiting for transfers between devices, on_device(): full_sorted = lax.all_gather(sorted_slab, 'orb', axis=3, tiled=True)  39.5 us
    all_gather x1, blocking collectives, on_device(): collision = lax.all_gather(summed_rows, 'orb', axis=1, tiled=True)  28.1 us
  transfers between devices with their start and end apart: 2, of which 2 were waited for; matrix products, arithmetic and copies ran while one was open for 1% of the time, Pallas kernels for 0%

commit v1 on v0

--- a/solution.py
+++ b/solution.py
@@ -129,7 +129,13 @@
     local_collision = history_terms(
         forward, back_full, weights, interaction, inter_rows, row_start, row_count
     )
-    summed_rows = lax.psum(local_collision, "tm")
+    size = lax.axis_size("tm")
+    summed_rows, far = (local_collision, 1)
+    while far < size:
+        summed_rows = summed_rows + lax.ppermute(
+            summed_rows, "tm", [(i, i ^ far) for i in range(size)]
+        )
+        far = 2 * far
     collision = lax.all_gather(summed_rows, "orb", axis=1, tiled=True)
     own_rows = lax.dynamic_slice_in_dim(collision, row_start, row_count, 1)
     own_columns = lax.dynamic_slice_in_dim(collision, row_start, row_count, 2)

time: 482 us -> 428 us (0.89)
  blocking collectives: 86.2 us -> 18.3 us
  waiting for transfers between devices: 95.1 us -> 105 us
    psum x1 -> x0, blocking collectives: 58.1 us -> none  [on_device(): summed_rows = lax.psum(local_collision, 'tm')]
    all_gather x1, blocking collectives: 28.1 us -> 18.3 us  [on_device(): collision = lax.all_gather(summed_rows, 'orb', axis=1, tiled=True)]
    ppermute x0 -> x4, waiting for transfers between devices: none -> 7.44 us  [on_device(): lax.ppermute(summed_rows, 'tm', [(i, i ^ far) for i in range(size)])]
  transfers between devices with their start and end apart: 2 -> 6, of which waited for: 2 -> 6; matrix products, arithmetic and copies ran while one was open for 1% -> 2% of each run, Pallas kernels for 0% -> 0%
where the time goes in v1:
time: 428 us; the launch traced here: 424 us
  matrix products  218 us (51%)
  waiting for transfers between devices  105 us (25%)
  local copies, waits for them, and re-layouts  46.3 us (11%)
  blocking collectives  18.3 us (4%)
  between operations  13.6 us (3%)
  other arithmetic  13.1 us (3%)
  starting transfers between devices  8.91 us (2%)
    all_to_all x1, waiting for transfers between devices, on_device(): lax.all_to_all(full_sorted, 'tm', split_axis=2, concat_axis=2, tiled=True)  58.5 us
    dot_general x24, matrix products, complex_einsum(): jnp.einsum(form, left_re, right_im, preferred_element_type=jnp.float32)  48.3 us
    dot_general x24, matrix products, complex_einsum(): jnp.einsum(form, left_im, right_im, preferred_element_type=jnp.float32)  48.2 us
    dot_general x24, matrix products, complex_einsum(): jnp.einsum(form, left_im, right_re, preferred_element_type=jnp.float32)  45 us
    dot_general x24, matrix products, complex_einsum(): jnp.einsum(form, left_re, right_re, preferred_element_type=jnp.float32)  44.8 us
    all_gather x1, waiting for transfers between devices, on_device(): full_sorted = lax.all_gather(sorted_slab, 'orb', axis=3, tiled=True)  39.5 us
    all_gather x1, blocking collectives, on_device(): collision = lax.all_gather(summed_rows, 'orb', axis=1, tiled=True)  18.3 us
    dot_general x8, matrix products, self_energy(): jnp.einsum('sik,kj->sij', left_re, interaction, preferred_element_type=jn...  16.2 us
  transfers between devices with their start and end apart: 6, of which 6 were waited for; matrix products, arithmetic and copies ran while one was open for 2% of the time, Pallas kernels for 0%

profile of v1, /device:TPU:1, one launch (start us, length us, event | category | flops | bytes accessed | tf_op | source)
XLA Modules:
  0.0 424.4 jit_solution(10098816386899053415)
XLA Ops:
  10.6 39.5 %all-gather.2.cloned.1.call-done = bf16[2,2,32,128,128]{4,3,1,0,2:T(8,128)(2,1)} async-done(((bf16[2,2,32,16,128]{4,3,1,0,2:T(8,128)(2,1)}), bf16[2,2,32,128,128]{4,3,1,0,2:T(8,128)(2,1)}) %all-gather.2.cloned.1.call-update) | async-done | bytes 4194320 | tf_op jit(solution)/shard_map/all_gather | solution.py:126
  50.1 6.6 %all-to-all-start = ((bf16[2,2,32,128,128]{4,3,1,0,2:T(8,128)(2,1)}), bf16[2,2,32,128,128]{4,3,1,0,2:T(8,128)(2,1)}, u32[]{:S(2)}, u32[]{:S(2)}) async-start(bf16[2,2,32,128,128]{4,3,1,0,2:T(8,128)(2,1)} %all-gather.2.cloned.1.call-done), calls=%async_computation | async-start | bytes 8388608 | tf_op jit(solution)/shard_map/all_to_all | solution.py:127
  61.1 58.5 %all-to-all-done = bf16[2,2,32,128,128]{4,3,1,0,2:T(8,128)(2,1)} async-done(((bf16[2,2,32,128,128]{4,3,1,0,2:T(8,128)(2,1)}), bf16[2,2,32,128,128]{4,3,1,0,2:T(8,128)(2,1)}, u32[]{:S(2)}, u32[]{:S(2)}) %all-to-all-start) | async-done | bytes 4194336 | tf_op jit(solution)/shard_map/all_to_all | solution.py:127
  119.6 4.7 %copy.45 = bf16[2,2,32,128,128]{4,3,2,1,0:T(8,128)(2,1)} copy(bf16[2,2,32,128,128]{4,3,1,0,2:T(8,128)(2,1)} %all-to-all-done) | data formatting | bytes 8388608 | tf_op jit(solution)/shard_map/all_to_all | solution.py:127
  124.3 5.2 %gather_fusion.1 = bf16[32,2,2,128,128]{4,3,2,1,0:T(8,128)(2,1)} fusion(bf16[2,2,32,128,128]{4,3,2,1,0:T(8,128)(2,1)} %copy.45, s32[1024]{0:T(1024)S(1)} %pad_clamp_fusion), kind=kCustom, calls=%fused_computation.1 | custom fusion | bytes 8388736 | tf_op jit(solution)/shard_map/jit(_take)/gather | solution.py:128
  129.5 4.6 %select_bitcast_fusion = bf16[2,2,32,128,128]{4,3,1,0,2:T(8,128)(2,1)} fusion(bf16[32,2,2,128,128]{4,3,2,1,0:T(8,128)(2,1)} %gather_fusion.1, pred[32]{0:T(512)(128)(4,1)S(1)} %compare_and_fusion.1), kind=kLoop, calls=%fused_computation.226 | loop fusion | flops 2097152 | bytes 8388640 | tf_op jit(solution)/shard_map/jit(_take)/select_n | solution.py:128
  134.1 249.0 %while.16 = (s32[]{:T(128)}, f32[2,16,128]{2,1,0:T(8,128)}, f32[32]{0:T(128)S(1)}, bf16[2,2,32,128,128]{4,3,2,1,0:T(8,128)(2,1)}, s32[]{:T(128)}, /*index=5*/bf1...) while((s32[]{:T(128)}, f32[2,16,128]{2,1,0:T(8,128)}, ...), condition=%wide.region_8.9_spmd.clone, body=%wide.region_3.8_spmd.clone.sunk | while | flops 4459808768 | bytes 142112496 | solution.py:97
  148.4 2.6 fusion.413
  153.3 2.3 fusion.414
  157.8 2.6 fusion.410
  162.7 2.3 fusion.411
  173.2 2.6 fusion.427
  178.1 2.3 fusion.428
  182.5 2.6 fusion.424
  187.5 2.3 fusion.425
  210.6 2.6 fusion.413
  215.5 2.3 fusion.414
  220.0 2.6 fusion.410
  224.9 2.3 fusion.411
  235.4 2.6 fusion.427
  240.3 2.3 fusion.428
  244.8 2.6 fusion.424
  272.9 2.6 fusion.413
  282.3 2.6 fusion.410
  297.6 2.6 fusion.427
  307.0 2.6 fusion.424
  335.1 2.6 fusion.413
  344.5 2.6 fusion.410
  359.9 2.6 fusion.427
  369.3 2.6 fusion.424
  388.3 2.4 collective-permute-done.1
  397.7 18.3 %all_gather.7 = f32[2,128,128]{2,1,0:T(8,128)S(1)} all-gather(f32[2,16,128]{2,1,0:T(8,128)S(1)} %add.230), channel_id=1, replica_groups=mesh['tm'=16,'orb'=8] {'orb'}, dimensions={1}, use_global_device_ids=true | all-gather | bytes 147456 | tf_op jit(solution)/shard_map/all_gather | solution.py:139
  (297 shorter events, 212.2 us)
Async XLA Ops:
  6.5 43.6 %all-gather.2.cloned.1.call-start = ((), (), s32[]{:S(2)}) async-start(), calls=%async_computation.1 | async-start | bytes 4718592 | tf_op jit(solution)/shard_map/all_gather | solution.py:126
  10.6 46.1 %copy-start.10 = (s32[512]{0:T(512)S(1)}, s32[512]{0:T(512)}, u32[]{:S(2)}) copy-start(s32[512]{0:T(512)} %param.11) | copy-start | bytes 6148
  50.1 69.5 %all-to-all-start = ((bf16[2,2,32,128,128]{4,3,1,0,2:T(8,128)(2,1)}), bf16[2,2,32,128,128]{4,3,1,0,2:T(8,128)(2,1)}, u32[]{:S(2)}, u32[]{:S(2)}) async-start(bf16[2,2,32,128,128]{4,3,1,0,2:T(8,128)(2,1)} %all-gather.2.cloned.1.call-done), calls=%async_computation | async-start | bytes 8388608 | tf_op jit(solution)/shard_map/all_to_all | solution.py:127
  134.1 6.7 %copy-start.2 = (bf16[128,128]{1,0:T(8,128)(2,1)}, bf16[128,128]{1,0:T(8,128)(2,1)S(1)}, u32[]{:S(2)}) copy-start(bf16[128,128]{1,0:T(8,128)(2,1)S(1)} %get-tuple-element.396) | copy-start | bytes 98308 | tf_op jit(solution)/shard_map/while
  160.4 4.5 %copy-start.5 = (f32[8,16,128]{2,1,0:T(8,128)S(1)}, f32[8,16,128]{2,1,0:T(8,128)}, u32[]{:S(2)}) copy-start(f32[8,16,128]{2,1,0:T(8,128)} %fusion.408) | copy-start | bytes 196612 | tf_op jit(solution)/shard_map/while
  185.2 4.5 %copy-start.3 = (bf16[128,128]{1,0:T(8,128)(2,1)S(1)}, bf16[128,128]{1,0:T(8,128)(2,1)}, u32[]{:S(2)}) copy-start(bf16[128,128]{1,0:T(8,128)(2,1)} %copy-done.2) | copy-start | bytes 98308 | tf_op jit(solution)/shard_map/while
  185.2 4.5 %copy-start.4 = (f32[8,16,128]{2,1,0:T(8,128)S(1)}, f32[8,16,128]{2,1,0:T(8,128)}, u32[]{:S(2)}) copy-start(f32[8,16,128]{2,1,0:T(8,128)} %fusion.422) | copy-start | bytes 196612 | tf_op jit(solution)/shard_map/while
  187.5 8.3 %copy-start.6 = (f32[2,16,128]{2,1,0:T(8,128)S(1)}, f32[2,16,128]{2,1,0:T(8,128)}, u32[]{:S(2)}) copy-start(f32[2,16,128]{2,1,0:T(8,128)} %get-tuple-element.377) | copy-start | bytes 49156 | tf_op jit(solution)/shard_map/while
  187.5 8.9 %copy-start.12 = (f32[32]{0:T(128)S(1)}, f32[32]{0:T(128)}, u32[]{:S(2)}) copy-start(f32[32]{0:T(128)} %copy-done.11) | copy-start | bytes 388 | tf_op jit(solution)/shard_map/while
  196.4 6.7 %copy-start.2 = (bf16[128,128]{1,0:T(8,128)(2,1)}, bf16[128,128]{1,0:T(8,128)(2,1)S(1)}, u32[]{:S(2)}) copy-start(bf16[128,128]{1,0:T(8,128)(2,1)S(1)} %get-tuple-element.396) | copy-start | bytes 98308 | tf_op jit(solution)/shard_map/while
  222.7 4.5 %copy-start.5 = (f32[8,16,128]{2,1,0:T(8,128)S(1)}, f32[8,16,128]{2,1,0:T(8,128)}, u32[]{:S(2)}) copy-start(f32[8,16,128]{2,1,0:T(8,128)} %fusion.408) | copy-start | bytes 196612 | tf_op jit(solution)/shard_map/while
  247.4 4.5 %copy-start.3 = (bf16[128,128]{1,0:T(8,128)(2,1)S(1)}, bf16[128,128]{1,0:T(8,128)(2,1)}, u32[]{:S(2)}) copy-start(bf16[128,128]{1,0:T(8,128)(2,1)} %copy-done.2) | copy-start | bytes 98308 | tf_op jit(solution)/shard_map/while
  247.4 4.5 %copy-start.4 = (f32[8,16,128]{2,1,0:T(8,128)S(1)}, f32[8,16,128]{2,1,0:T(8,128)}, u32[]{:S(2)}) copy-start(f32[8,16,128]{2,1,0:T(8,128)} %fusion.422) | copy-start | bytes 196612 | tf_op jit(solution)/shard_map/while
  249.7 8.3 %copy-start.6 = (f32[2,16,128]{2,1,0:T(8,128)S(1)}, f32[2,16,128]{2,1,0:T(8,128)}, u32[]{:S(2)}) copy-start(f32[2,16,128]{2,1,0:T(8,128)} %get-tuple-element.377) | copy-start | bytes 49156 | tf_op jit(solution)/shard_map/while
  249.7 8.9 %copy-start.12 = (f32[32]{0:T(128)S(1)}, f32[32]{0:T(128)}, u32[]{:S(2)}) copy-start(f32[32]{0:T(128)} %copy-done.11) | copy-start | bytes 388 | tf_op jit(solution)/shard_map/while
  258.6 6.7 %copy-start.2 = (bf16[128,128]{1,0:T(8,128)(2,1)}, bf16[128,128]{1,0:T(8,128)(2,1)S(1)}, u32[]{:S(2)}) copy-start(bf16[128,128]{1,0:T(8,128)(2,1)S(1)} %get-tuple-element.396) | copy-start | bytes 98308 | tf_op jit(solution)/shard_map/while
  284.9 4.5 %copy-start.5 = (f32[8,16,128]{2,1,0:T(8,128)S(1)}, f32[8,16,128]{2,1,0:T(8,128)}, u32[]{:S(2)}) copy-start(f32[8,16,128]{2,1,0:T(8,128)} %fusion.408) | copy-start | bytes 196612 | tf_op jit(solution)/shard_map/while
  309.7 4.5 %copy-start.3 = (bf16[128,128]{1,0:T(8,128)(2,1)S(1)}, bf16[128,128]{1,0:T(8,128)(2,1)}, u32[]{:S(2)}) copy-start(bf16[128,128]{1,0:T(8,128)(2,1)} %copy-done.2) | copy-start | bytes 98308 | tf_op jit(solution)/shard_map/while
  309.7 4.5 %copy-start.4 = (f32[8,16,128]{2,1,0:T(8,128)S(1)}, f32[8,16,128]{2,1,0:T(8,128)}, u32[]{:S(2)}) copy-start(f32[8,16,128]{2,1,0:T(8,128)} %fusion.422) | copy-start | bytes 196612 | tf_op jit(solution)/shard_map/while
  311.9 8.3 %copy-start.6 = (f32[2,16,128]{2,1,0:T(8,128)S(1)}, f32[2,16,128]{2,1,0:T(8,128)}, u32[]{:S(2)}) copy-start(f32[2,16,128]{2,1,0:T(8,128)} %get-tuple-element.377) | copy-start | bytes 49156 | tf_op jit(solution)/shard_map/while
  311.9 8.9 %copy-start.12 = (f32[32]{0:T(128)S(1)}, f32[32]{0:T(128)}, u32[]{:S(2)}) copy-start(f32[32]{0:T(128)} %copy-done.11) | copy-start | bytes 388 | tf_op jit(solution)/shard_map/while
  320.8 6.7 %copy-start.2 = (bf16[128,128]{1,0:T(8,128)(2,1)}, bf16[128,128]{1,0:T(8,128)(2,1)S(1)}, u32[]{:S(2)}) copy-start(bf16[128,128]{1,0:T(8,128)(2,1)S(1)} %get-tuple-element.396) | copy-start | bytes 98308 | tf_op jit(solution)/shard_map/while
  347.1 4.5 %copy-start.5 = (f32[8,16,128]{2,1,0:T(8,128)S(1)}, f32[8,16,128]{2,1,0:T(8,128)}, u32[]{:S(2)}) copy-start(f32[8,16,128]{2,1,0:T(8,128)} %fusion.408) | copy-start | bytes 196612 | tf_op jit(solution)/shard_map/while
  371.9 4.5 %copy-start.3 = (bf16[128,128]{1,0:T(8,128)(2,1)S(1)}, bf16[128,128]{1,0:T(8,128)(2,1)}, u32[]{:S(2)}) copy-start(bf16[128,128]{1,0:T(8,128)(2,1)} %copy-done.2) | copy-start | bytes 98308 | tf_op jit(solution)/shard_map/while
  371.9 4.5 %copy-start.4 = (f32[8,16,128]{2,1,0:T(8,128)S(1)}, f32[8,16,128]{2,1,0:T(8,128)}, u32[]{:S(2)}) copy-start(f32[8,16,128]{2,1,0:T(8,128)} %fusion.422) | copy-start | bytes 196612 | tf_op jit(solution)/shard_map/while
  374.2 8.3 %copy-start.6 = (f32[2,16,128]{2,1,0:T(8,128)S(1)}, f32[2,16,128]{2,1,0:T(8,128)}, u32[]{:S(2)}) copy-start(f32[2,16,128]{2,1,0:T(8,128)} %get-tuple-element.377) | copy-start | bytes 49156 | tf_op jit(solution)/shard_map/while
  374.2 8.9 %copy-start.12 = (f32[32]{0:T(128)S(1)}, f32[32]{0:T(128)}, u32[]{:S(2)}) copy-start(f32[32]{0:T(128)} %copy-done.11) | copy-start | bytes 388 | tf_op jit(solution)/shard_map/while
  383.1 34.5 %copy-start.1 = (bf16[2,2,32,16,128]{4,3,2,1,0:T(8,128)(2,1)S(1)}, bf16[2,2,32,16,128]{4,3,2,1,0:T(8,128)(2,1)}, u32[]{:S(2)}) copy-start(bf16[2,2,32,16,128]{4,3,2,1,0:T(8,128)(2,1)} %param.10) | copy-start | bytes 1572868
  383.1 2.8 collective-permute-start
  386.6 4.1 collective-permute-start.1
  390.7 2.9 collective-permute-start.2
  393.6 4.1 collective-permute-start.3
  (11 other events, 9.1 us)
Sparse Core Ops, SparseCore 0:
  10.7 39.3 all-gather.1
